TPU v7x, 128 devices: a whole 4x4x4 slice. The times are simulated.
128 devices in a mesh: dom: 32 (over y, x, core), near: 4 (over z).
Axes of the slice: x: 4, y: 4, z: 4, core: 2. Of those that a mesh axis runs over, the one named last changes fastest.
Arguments:
- start_block: float32 [131072, 128], P(('dom', 'near')), may hold values from -6 to 6
- near_tiles: float32 [6144, 128, 128], P(('dom', 'near')), may hold values from -0.09375 to 0.09375
- near_src: int32 [6144], P(('dom', 'near')), may hold values from 0 to 31, as said below
- near_mask: int32 [6144], P(('dom', 'near')), may hold values 0 or 1
- far_tiles: float32 [1024, 128, 128], P(('dom', 'near')), may hold values from -0.09375 to 0.09375
- far_src: int32 [1024], P(('dom', 'near')), may hold values from 0 to 31
- far_mask: int32 [1024], P(('dom', 'near')), may hold values 0 or 1
- bound_count: int32 [128], P(('dom', 'near')), may hold values from 1 to 128
Outputs:
- encodings: float32 [131072, 128], P(('dom', 'near'))
- rayleigh: float32 [128, 128], replicated
Inputs may be any that keep to these rules, and one draw needn't show every extreme that they name: `near_src`: each partition holds 48 consecutive slots; the slot at position j among them (j from 0) lies in tile row j // 6; the first slot of each tile row reads the partition's own tile of that row; every source tile from another partition of the group is one of that partition's first 4 tiles.
All inputs are finite; a program needn't handle non-finite values. No bound on the sum of `near_mask` or of `far_mask` on one device may be relied on, other than what follows from the above.
Results may differ from a plain program's by a relative error of at most 0.0003.
Values sent between devices are 32-bit elements; how exact they have to be, the bound alone decides.
No kernel may reach another device: no remote copies, remote signals or barrier semaphores. Data moves between devices by JAX's collectives and lax.ppermute only.
A program may use at most 64 MiB of HBM per device.

v0:
```python
from functools import partial
import jax
import jax.numpy as jnp
from jax import lax
from jax.sharding import PartitionSpec as P

NPER = 6
ITERS = 2
DEG = 3
LOWER_EDGE = 0.6
UPPER_EDGE = 2.0


def apply_operator(
    block, near_tiles, near_src, near_mask, far_tiles, far_src, far_mask, bound_count
):
    tile_rows = near_tiles.shape[1]
    width = block.shape[1]
    tiles_dev = block.shape[0] // tile_rows
    group_size = lax.axis_size("near")
    gathered = lax.all_gather(block, "near", axis=0, tiled=True)
    picked = gathered.reshape(group_size * tiles_dev, tile_rows, width)[near_src]
    products = jnp.einsum("sij,sjk->sik", near_tiles, picked, precision=lax.Precision.HIGHEST)
    products = products * near_mask.astype(jnp.float32)[:, None, None]
    near_sum = products.reshape(tiles_dev, NPER, tile_rows, width).sum(axis=1)
    limit = (jnp.arange(tile_rows) < bound_count[0]).astype(jnp.float32)
    edge_tile = block[:tile_rows] * limit[:, None]
    edges = lax.all_gather(edge_tile, "dom", axis=0, tiled=True).reshape(
        lax.axis_size("dom"), tile_rows, width
    )
    far_pick = edges[far_src]
    far_sum = jnp.einsum("sij,sjk->sik", far_tiles, far_pick, precision=lax.Precision.HIGHEST)
    far_sum = far_sum * far_mask.astype(jnp.float32)[:, None, None]
    return block - (near_sum + far_sum).reshape(block.shape)


def chebyshev(current, image, operator):
    center = (UPPER_EDGE + LOWER_EDGE) / 2.0
    half = (UPPER_EDGE - LOWER_EDGE) / 2.0
    previous = current
    present = (image - center * current) / half
    for degree in range(DEG - 1):
        following = 2.0 * (operator(present) - center * present) / half - previous
        previous, present = (present, following)
    return present


def inner(left, right):
    return jnp.dot(
        left.T, right, precision=lax.Precision.HIGHEST, preferred_element_type=jnp.float32
    )


def times_inverse(block, lower_inv):
    return jnp.dot(
        block, lower_inv.T, precision=lax.Precision.HIGHEST, preferred_element_type=jnp.float32
    )


def inverse_factor(gram):
    lower = jnp.linalg.cholesky(gram)
    return jax.scipy.linalg.solve_triangular(
        lower, jnp.eye(gram.shape[0], dtype=jnp.float32), lower=True
    )


def local(start_block, near_tiles, near_src, near_mask, far_tiles, far_src, far_mask, bound_count):
    operator = partial(
        apply_operator,
        near_tiles=near_tiles,
        near_src=near_src,
        near_mask=near_mask,
        far_tiles=far_tiles,
        far_src=far_src,
        far_mask=far_mask,
        bound_count=bound_count,
    )
    nodes_all = start_block.shape[0] * lax.axis_size("dom") * lax.axis_size("near")
    current = start_block
    image = operator(current)
    for iteration in range(ITERS):
        if iteration > 0:
            image = operator(current)
        filtered = chebyshev(current, image, operator)
        gram = lax.psum(inner(filtered, filtered), ("dom", "near")) / nodes_all
        lower_inv = inverse_factor(gram)
        current = times_inverse(filtered, lower_inv)
    final_image = operator(current)
    rayleigh = lax.psum(inner(current, final_image), ("dom", "near")) / nodes_all
    return (current, rayleigh)


def solution(mesh):
    return jax.shard_map(
        local,
        mesh=mesh,
        in_specs=(
            P(("dom", "near"), None),
            P(("dom", "near"), None, None),
            P(("dom", "near")),
            P(("dom", "near")),
            P(("dom", "near"), None, None),
            P(("dom", "near")),
            P(("dom", "near")),
            P(("dom", "near")),
        ),
        out_specs=(P(("dom", "near"), None), P()),
        check_vma=False,
    )
```

profile of v0, /device:TPU:1, one launch (start us, length us, event | category | flops | bytes accessed | tf_op | source)
XLA Modules:
  0.0 1082.7 jit_solution(1137057290617790462)
XLA Ops:
  13.1 30.7 %all-gather.15.cloned.1.call-done = f32[4096,128]{1,0:T(8,128)} async-done(((f32[1024,128]{1,0:T(8,128)}), f32[4096,128]{1,0:T(8,128)}) %all-gather.15.cloned.1.call-update) | async-done | bytes 2097168 | tf_op jit(solution)/shard_map/all_gather | solution.py:21
  43.7 4.0 gather_fusion
  47.7 8.1 convolution_multiply_fusion.6
  60.8 29.6 %all-gather.17.cloned.1.call-done = f32[4096,128]{1,0:T(8,128)} async-done(((f32[128,128]{1,0:T(8,128)}), f32[4096,128]{1,0:T(8,128)}) %all-gather.17.cloned.1.call-update) | async-done | bytes 2097168 | tf_op jit(solution)/shard_map/all_gather | solution.py:28
  90.4 3.0 gather_fusion.1
  99.8 28.3 %all-gather.19.cloned.1.call-done = f32[4096,128]{1,0:T(8,128)} async-done(((f32[1024,128]{1,0:T(8,128)}), f32[4096,128]{1,0:T(8,128)}) %all-gather.19.cloned.1.call-update) | async-done | bytes 2097168 | tf_op jit(solution)/shard_map/all_gather | solution.py:21
  128.1 4.0 gather_fusion.2
  132.1 8.1 convolution_multiply_fusion.5
  140.2 3.0 reduce_sum.64
  145.2 29.5 %all-gather.21.cloned.1.call-done = f32[4096,128]{1,0:T(8,128)} async-done(((f32[128,128]{1,0:T(8,128)}), f32[4096,128]{1,0:T(8,128)}) %all-gather.21.cloned.1.call-update) | async-done | bytes 2097168 | tf_op jit(solution)/shard_map/all_gather | solution.py:28
  174.7 3.0 gather_fusion.3
  184.5 28.1 %all-gather.23.cloned.1.call-done = f32[4096,128]{1,0:T(8,128)} async-done(((f32[1024,128]{1,0:T(8,128)}), f32[4096,128]{1,0:T(8,128)}) %all-gather.23.cloned.1.call-update) | async-done | bytes 2097168 | tf_op jit(solution)/shard_map/all_gather | solution.py:21
  212.6 4.0 gather_fusion.4
  216.5 8.1 convolution_multiply_fusion.4
  224.7 3.0 reduce_sum.65
  229.7 29.5 %all-gather.25.cloned.1.call-done = f32[4096,128]{1,0:T(8,128)} async-done(((f32[128,128]{1,0:T(8,128)}), f32[4096,128]{1,0:T(8,128)}) %all-gather.25.cloned.1.call-update) | async-done | bytes 2097168 | tf_op jit(solution)/shard_map/all_gather | solution.py:28
  259.1 3.0 gather_fusion.5
  268.2 138.8 %all-reduce.4.cloned.1.call-done = f32[128,128]{0,1:T(8,128)} async-done(((f32[128,128]{0,1:T(8,128)}), f32[128,128]{0,1:T(8,128)}) %all-reduce.4.cloned.1.call-update) | async-done | bytes 65552 | tf_op jit(solution)/shard_map/psum | solution.py:85
  408.8 11.7 %cholesky.44 = f32[128,128]{1,0:T(8,128)S(1)} custom-call(f32[128,128]{1,0:T(8,128)S(1)} %fusion.41), custom_call_target="Cholesky" | custom-call | tf_op jit(solution)/shard_map/jit(cholesky)/cholesky | solution.py:61
  421.9 9.8 custom-call.6
  436.1 26.2 %all-gather.27.cloned.1.call-done = f32[4096,128]{1,0:T(8,128)} async-done(((f32[1024,128]{1,0:T(8,128)}), f32[4096,128]{1,0:T(8,128)}) %all-gather.27.cloned.1.call-update) | async-done | bytes 2097168 | tf_op jit(solution)/shard_map/all_gather | solution.py:21
  462.3 4.0 gather_fusion.6
  466.3 8.1 convolution_multiply_fusion.3
  474.4 2.9 reduce_sum.66
  479.4 29.6 %all-gather.29.cloned.1.call-done = f32[4096,128]{1,0:T(8,128)} async-done(((f32[128,128]{1,0:T(8,128)}), f32[4096,128]{1,0:T(8,128)}) %all-gather.29.cloned.1.call-update) | async-done | bytes 2097168 | tf_op jit(solution)/shard_map/all_gather | solution.py:28
  509.0 3.0 gather_fusion.7
  518.6 28.1 %all-gather.31.cloned.1.call-done = f32[4096,128]{1,0:T(8,128)} async-done(((f32[1024,128]{1,0:T(8,128)}), f32[4096,128]{1,0:T(8,128)}) %all-gather.31.cloned.1.call-update) | async-done | bytes 2097168 | tf_op jit(solution)/shard_map/all_gather | solution.py:21
  546.7 4.0 gather_fusion.8
  550.7 8.1 convolution_multiply_fusion.2
  558.8 2.9 reduce_sum.67
  563.8 29.6 %all-gather.33.cloned.1.call-done = f32[4096,128]{1,0:T(8,128)} async-done(((f32[128,128]{1,0:T(8,128)}), f32[4096,128]{1,0:T(8,128)}) %all-gather.33.cloned.1.call-update) | async-done | bytes 2097168 | tf_op jit(solution)/shard_map/all_gather | solution.py:28
  593.4 3.0 gather_fusion.9
  603.0 28.3 %all-gather.35.cloned.1.call-done = f32[4096,128]{1,0:T(8,128)} async-done(((f32[1024,128]{1,0:T(8,128)}), f32[4096,128]{1,0:T(8,128)}) %all-gather.35.cloned.1.call-update) | async-done | bytes 2097168 | tf_op jit(solution)/shard_map/all_gather | solution.py:21
  631.3 4.0 gather_fusion.10
  635.3 8.1 convolution_multiply_fusion.1
  643.4 2.9 reduce_sum.68
  648.4 29.6 %all-gather.37.cloned.1.call-done = f32[4096,128]{1,0:T(8,128)} async-done(((f32[128,128]{1,0:T(8,128)}), f32[4096,128]{1,0:T(8,128)}) %all-gather.37.cloned.1.call-update) | async-done | bytes 2097168 | tf_op jit(solution)/shard_map/all_gather | solution.py:28
  678.0 3.0 gather_fusion.11
  687.5 138.4 %all-reduce.6.cloned.1.call-done = f32[128,128]{0,1:T(8,128)} async-done(((f32[128,128]{0,1:T(8,128)}), f32[128,128]{0,1:T(8,128)}) %all-reduce.6.cloned.1.call-update) | async-done | bytes 65552 | tf_op jit(solution)/shard_map/psum | solution.py:85
  827.7 11.7 %cholesky.55 = f32[128,128]{1,0:T(8,128)S(1)} custom-call(f32[128,128]{1,0:T(8,128)S(1)} %fusion.39), custom_call_target="Cholesky" | custom-call | tf_op jit(solution)/shard_map/jit(cholesky)/cholesky | solution.py:61
  840.8 9.8 custom-call.7
  855.2 26.0 %all-gather.39.cloned.1.call-done = f32[4096,128]{1,0:T(8,128)} async-done(((f32[1024,128]{1,0:T(8,128)}), f32[4096,128]{1,0:T(8,128)}) %all-gather.39.cloned.1.call-update) | async-done | bytes 2097168 | tf_op jit(solution)/shard_map/all_gather | solution.py:21
  881.2 4.0 gather_fusion.12
  885.2 8.1 convolution_multiply_fusion
  893.3 3.0 reduce_sum.69
  898.3 29.5 %all-gather.41.cloned.1.call-done = f32[4096,128]{1,0:T(8,128)} async-done(((f32[128,128]{1,0:T(8,128)}), f32[4096,128]{1,0:T(8,128)}) %all-gather.41.cloned.1.call-update) | async-done | bytes 2097168 | tf_op jit(solution)/shard_map/all_gather | solution.py:28
  927.7 3.0 gather_fusion.13
  935.5 138.9 %all-reduce.8.cloned.1.call-done = f32[128,128]{0,1:T(8,128)} async-done(((f32[128,128]{0,1:T(8,128)}), f32[128,128]{0,1:T(8,128)}) %all-reduce.8.cloned.1.call-update) | async-done | bytes 65552 | tf_op jit(solution)/shard_map/psum | solution.py:89
  (104 shorter events, 82.7 us)
Async XLA Ops:
  7.2 40.5 %copy-start = (f32[48,128,128]{2,1,0:T(8,128)S(1)}, f32[48,128,128]{2,1,0:T(8,128)}, u32[]{:S(2)}) copy-start(f32[48,128,128]{2,1,0:T(8,128)} %param.12) | copy-start | bytes 9437188
  7.2 36.5 %all-gather.15.cloned.1.call-start = ((), (), s32[]{:S(2)}) async-start(), calls=%async_computation | async-start | bytes 2621440 | tf_op jit(solution)/shard_map/all_gather | solution.py:21
  7.9 82.5 %all-gather.17.cloned.1.call-start = ((), (), s32[]{:S(2)}) async-start(), calls=%async_computation.1 | async-start | bytes 2162688 | tf_op jit(solution)/shard_map/all_gather | solution.py:28
  10.4 117.7 %all-gather.19.cloned.1.call-start = ((), (), s32[]{:S(2)}) async-start(), calls=%async_computation.2 | async-start | bytes 2621440 | tf_op jit(solution)/shard_map/all_gather | solution.py:21
  95.4 0.8 copy-start.2
  98.1 76.5 %all-gather.21.cloned.1.call-start = ((), (), s32[]{:S(2)}) async-start(), calls=%async_computation.3 | async-start | bytes 2162688 | tf_op jit(solution)/shard_map/all_gather | solution.py:28
  99.8 112.8 %all-gather.23.cloned.1.call-start = ((), (), s32[]{:S(2)}) async-start(), calls=%async_computation.4 | async-start | bytes 2621440 | tf_op jit(solution)/shard_map/all_gather | solution.py:21
  179.6 0.8 copy-start.6
  182.6 76.5 %all-gather.25.cloned.1.call-start = ((), (), s32[]{:S(2)}) async-start(), calls=%async_computation.5 | async-start | bytes 2162688 | tf_op jit(solution)/shard_map/all_gather | solution.py:28
  184.2 222.8 %all-reduce.4.cloned.1.call-start = ((), (), s32[]{:S(2)}) async-start(), calls=%async_computation.6 | async-start | bytes 131072 | tf_op jit(solution)/shard_map/psum | solution.py:85
  265.7 0.8 copy-start.4
  268.1 194.2 %all-gather.27.cloned.1.call-start = ((), (), s32[]{:S(2)}) async-start(), calls=%async_computation.7 | async-start | bytes 2621440 | tf_op jit(solution)/shard_map/all_gather | solution.py:21
  434.5 74.6 %all-gather.29.cloned.1.call-start = ((), (), s32[]{:S(2)}) async-start(), calls=%async_computation.8 | async-start | bytes 2162688 | tf_op jit(solution)/shard_map/all_gather | solution.py:28
  436.1 110.6 %all-gather.31.cloned.1.call-start = ((), (), s32[]{:S(2)}) async-start(), calls=%async_computation.9 | async-start | bytes 2621440 | tf_op jit(solution)/shard_map/all_gather | solution.py:21
  514.0 0.8 copy-start.1
  516.7 76.7 %all-gather.33.cloned.1.call-start = ((), (), s32[]{:S(2)}) async-start(), calls=%async_computation.10 | async-start | bytes 2162688 | tf_op jit(solution)/shard_map/all_gather | solution.py:28
  518.4 112.9 %all-gather.35.cloned.1.call-start = ((), (), s32[]{:S(2)}) async-start(), calls=%async_computation.11 | async-start | bytes 2621440 | tf_op jit(solution)/shard_map/all_gather | solution.py:21
  598.3 0.8 copy-start.5
  601.3 76.7 %all-gather.37.cloned.1.call-start = ((), (), s32[]{:S(2)}) async-start(), calls=%async_computation.12 | async-start | bytes 2162688 | tf_op jit(solution)/shard_map/all_gather | solution.py:28
  603.0 223.0 %all-reduce.6.cloned.1.call-start = ((), (), s32[]{:S(2)}) async-start(), calls=%async_computation.13 | async-start | bytes 131072 | tf_op jit(solution)/shard_map/psum | solution.py:85
  684.6 0.8 copy-start.3
  687.0 194.1 %all-gather.39.cloned.1.call-start = ((), (), s32[]{:S(2)}) async-start(), calls=%async_computation.14 | async-start | bytes 2621440 | tf_op jit(solution)/shard_map/all_gather | solution.py:21
  853.3 74.4 %all-gather.41.cloned.1.call-start = ((), (), s32[]{:S(2)}) async-start(), calls=%async_computation.15 | async-start | bytes 2162688 | tf_op jit(solution)/shard_map/all_gather | solution.py:28
  855.0 219.5 %all-reduce.8.cloned.1.call-start = ((), (), s32[]{:S(2)}) async-start(), calls=%async_computation.16 | async-start | bytes 131072 | tf_op jit(solution)/shard_map/psum | solution.py:89
Sparse Core Ops, SparseCore 0:
  9.6 34.0 all-gather.14
  46.5 43.8 all-gather.16
  98.3 29.7 all-gather.18
  130.8 43.8 all-gather.20
  182.7 29.7 all-gather.22
  215.2 43.8 all-gather.24
  268.3 138.7 all-reduce.3
  434.6 27.6 all-gather.26
  465.1 43.8 all-gather.28
  516.9 29.7 all-gather.30
  549.5 43.8 all-gather.32
  601.5 29.7 all-gather.34
  634.1 43.8 all-gather.36
  687.1 138.7 all-reduce.5
  853.4 27.6 all-gather.38
  883.9 43.8 all-gather.40
  935.7 138.7 all-reduce.7
where the time goes:
time: 1090 us; the launch traced here: 1080 us
  waiting for transfers between devices  819 us (75%)
  other arithmetic  95.5 us (9%)
  matrix products  82.2 us (8%)
  local copies, waits for them, and re-layouts  68.7 us (6%)
  between operations  15.2 us (1%)
    psum x2, waiting for transfers between devices, local(): gram = lax.psum(inner(filtered, filtered), ('dom', 'near')) / nodes_all  277 us
    all_gather x7, waiting for transfers between devices, apply_operator(): lax.all_gather(edge_tile, 'dom', axis=0, tiled=True)  207 us
    all_gather x7, waiting for transfers between devices, apply_operator(): gathered = lax.all_gather(block, 'near', axis=0, tiled=True)  196 us
    psum x1, waiting for transfers between devices, local(): lax.psum(inner(current, final_image), ('dom', 'near')) / nodes_all  139 us
    dot_general x7, matrix products, apply_operator(): jnp.einsum('sij,sjk->sik', near_tiles, picked, precision=lax.Precision.HI...  56.9 us
    gather x7, local copies, waits for them, and re-layouts, apply_operator(): gathered.reshape(group_size * tiles_dev, tile_rows, width)[near_src]  28 us
    another operation x6, other arithmetic, inverse_factor(): lower = jnp.linalg.cholesky(gram)  24.8 us
  transfers between devices with their start and end apart: 17, of which 17 were waited for; matrix products, arithmetic and copies ran while one was open for 12% of the time, Pallas kernels for 0%

commit v1 on v0

--- a/solution.py
+++ b/solution.py
@@ -3,6 +3,7 @@
 import jax.numpy as jnp
 from jax import lax
 from jax.sharding import PartitionSpec as P
+from jax.lax import all_to_all, axis_size
 
 NPER = 6
 ITERS = 2
@@ -18,7 +19,16 @@
     width = block.shape[1]
     tiles_dev = block.shape[0] // tile_rows
     group_size = lax.axis_size("near")
-    gathered = lax.all_gather(block, "near", axis=0, tiled=True)
+
+    def _direct_heads(w_in):
+        buffer = []
+        for _ in range(axis_size("near")):
+            buffer.append(w_in)
+        return jnp.concatenate(
+            all_to_all(jnp.stack(buffer), concat_axis=0, axis_name="near", split_axis=0), axis=0
+        )
+
+    gathered = _direct_heads(block)
     picked = gathered.reshape(group_size * tiles_dev, tile_rows, width)[near_src]
     products = jnp.einsum("sij,sjk->sik", near_tiles, picked, precision=lax.Precision.HIGHEST)
     products = products * near_mask.astype(jnp.float32)[:, None, None]

time: 1090 us -> 895 us (0.82)
  waiting for transfers between devices: 819 us -> 443 us
  blocking collectives: 0 us -> 172 us
  local copies, waits for them, and re-layouts: 68.7 us -> 83.2 us
  other arithmetic: 95.5 us -> 84.6 us
    all_gather x7, waiting for transfers between devices: 207 us -> 0.68 us  [apply_operator(): lax.all_gather(edge_tile, 'dom', axis=0, tiled=True)]
    all_gather x7 -> x0, waiting for transfers between devices: 196 us -> none  [apply_operator(): gathered = lax.all_gather(block, 'near', axis=0, tiled=True)]
    all_to_all x0 -> x6, blocking collectives: none -> 172 us  [_direct_heads(): all_to_all(jnp.stack(buffer), concat_axis=0, axis_name='near', split_axis=0)]
    all_to_all x0 -> x1, waiting for transfers between devices: none -> 25.6 us  [_direct_heads(): all_to_all(jnp.stack(buffer), concat_axis=0, axis_name='near', split_axis=0)]
  transfers between devices with their start and end apart: 17 -> 11, of which waited for: 17 -> 5; matrix products, arithmetic and copies ran while one was open for 12% -> 15% of each run, Pallas kernels for 0% -> 0%
where the time goes in v1:
time: 895 us; the launch traced here: 886 us
  waiting for transfers between devices  443 us (49%)
  blocking collectives  172 us (19%)
  other arithmetic  84.6 us (9%)
  local copies, waits for them, and re-layouts  83.2 us (9%)
  matrix products  80.6 us (9%)
  between operations  15.6 us (2%)
    psum x2, waiting for transfers between devices, local(): gram = lax.psum(inner(filtered, filtered), ('dom', 'near')) / nodes_all  280 us
    all_to_all x6, blocking collectives, _direct_heads(): all_to_all(jnp.stack(buffer), concat_axis=0, axis_name='near', split_axis=0)  172 us
    psum x1, waiting for transfers between devices, local(): lax.psum(inner(current, final_image), ('dom', 'near')) / nodes_all  137 us
    dot_general x7, matrix products, apply_operator(): jnp.einsum('sij,sjk->sik', near_tiles, picked, precision=lax.Precision.HI...  57 us
    gather x7, local copies, waits for them, and re-layouts, apply_operator(): gathered.reshape(group_size * tiles_dev, tile_rows, width)[near_src]  28.2 us
    all_to_all x1, waiting for transfers between devices, _direct_heads(): all_to_all(jnp.stack(buffer), concat_axis=0, axis_name='near', split_axis=0)  25.6 us
    another operation x6, other arithmetic, inverse_factor(): lower = jnp.linalg.cholesky(gram)  24.8 us
    another operation x4, other arithmetic, inverse_factor(): jax.scipy.linalg.solve_triangular(lower, jnp.eye(gram.shape[0], dtype=jnp...  20.9 us
  transfers between devices with their start and end apart: 11, of which 5 were waited for; matrix products, arithmetic and copies ran while one was open for 15% of the time, Pallas kernels for 0%

profile of v1, /device:TPU:1, one launch (start us, length us, event | category | flops | bytes accessed | tf_op | source)
XLA Modules:
  0.0 885.5 jit_solution(9739032829857342535)
XLA Ops:
  9.8 2.5 stack.14
  12.3 5.8 all-to-all-start
  18.2 25.6 %all-to-all-done = f32[4,1024,128]{2,1,0:T(8,128)} async-done(((f32[4,1024,128]{2,1,0:T(8,128)}), f32[4,1024,128]{2,1,0:T(8,128)}, u32[]{:S(2)}, u32[]{:S(2)}) %all-to-all-start) | async-done | bytes 2097184 | tf_op jit(solution)/shard_map/all_to_all | solution.py:28
  43.8 4.0 gather_fusion
  47.8 8.1 convolution_multiply_fusion.6
  55.9 2.9 reduce_sum.63
  58.9 2.0 copy.30
  60.9 3.0 gather_fusion.1
  70.5 27.8 %all_to_all.35 = f32[4,1024,128]{2,1,0:T(8,128)} all-to-all(f32[4,1024,128]{2,1,0:T(8,128)S(1)} %stack.15), channel_id=1, replica_groups=mesh['dom'=32,'near'=4] {'near'}, dimensions={0} | all-to-all | bytes 4194304 | tf_op jit(solution)/shard_map/all_to_all | solution.py:28
  98.3 4.0 gather_fusion.2
  102.3 8.1 convolution_multiply_fusion.5
  110.4 2.9 reduce_sum.64
  115.4 3.0 gather_fusion.3
  125.3 26.7 %all_to_all.36 = f32[4,1024,128]{2,1,0:T(8,128)} all-to-all(f32[4,1024,128]{2,1,0:T(8,128)S(1)} %stack.16), channel_id=1, replica_groups=mesh['dom'=32,'near'=4] {'near'}, dimensions={0} | all-to-all | bytes 4194304 | tf_op jit(solution)/shard_map/all_to_all | solution.py:28
  152.0 4.0 gather_fusion.4
  156.0 8.1 convolution_multiply_fusion.4
  164.1 2.9 reduce_sum.65
  167.1 2.0 copy.34
  169.8 3.0 gather_fusion.5
  178.8 142.0 %all-reduce.4.cloned.1.call-done = f32[128,128]{0,1:T(8,128)} async-done(((f32[128,128]{0,1:T(8,128)}), f32[128,128]{0,1:T(8,128)}) %all-reduce.4.cloned.1.call-update) | async-done | bytes 65552 | tf_op jit(solution)/shard_map/psum | solution.py:95
  322.6 11.7 %cholesky.44 = f32[128,128]{1,0:T(8,128)S(1)} custom-call(f32[128,128]{1,0:T(8,128)S(1)} %fusion.41), custom_call_target="Cholesky" | custom-call | tf_op jit(solution)/shard_map/jit(cholesky)/cholesky | solution.py:71
  335.6 9.8 %custom-call.6 = f32[1,128,128]{1,2,0:T(8,128)S(1)} custom-call(f32[1,128,128]{2,1,0:T(8,128)S(1)} %fusion.36), custom_call_target="InvertDiagBlocksLowerTriangular" | custom-call | tf_op jit(solution)/shard_map/jit(_solve_triangular)/triangular_solve | solution.py:72
  350.1 29.5 %all_to_all.37 = f32[4,1024,128]{2,1,0:T(8,128)} all-to-all(f32[4,1024,128]{2,1,0:T(8,128)S(1)} %stack.17), channel_id=1, replica_groups=mesh['dom'=32,'near'=4] {'near'}, dimensions={0} | all-to-all | bytes 4194304 | tf_op jit(solution)/shard_map/all_to_all | solution.py:28
  379.7 4.1 gather_fusion.6
  383.7 8.2 convolution_multiply_fusion.3
  391.9 2.9 reduce_sum.66
  396.9 3.0 gather_fusion.7
  406.5 29.6 %all_to_all.38 = f32[4,1024,128]{2,1,0:T(8,128)} all-to-all(f32[4,1024,128]{2,1,0:T(8,128)S(1)} %stack.18), channel_id=1, replica_groups=mesh['dom'=32,'near'=4] {'near'}, dimensions={0} | all-to-all | bytes 4194304 | tf_op jit(solution)/shard_map/all_to_all | solution.py:28
  436.1 4.1 gather_fusion.8
  440.2 8.2 convolution_multiply_fusion.2
  448.4 2.9 reduce_sum.67
  451.3 2.0 copy.40
  453.3 3.0 gather_fusion.9
  463.2 28.6 %all_to_all.39 = f32[4,1024,128]{2,1,0:T(8,128)} all-to-all(f32[4,1024,128]{2,1,0:T(8,128)S(1)} %stack.19), channel_id=1, replica_groups=mesh['dom'=32,'near'=4] {'near'}, dimensions={0} | all-to-all | bytes 4194304 | tf_op jit(solution)/shard_map/all_to_all | solution.py:28
  491.8 4.0 gather_fusion.10
  495.8 8.1 convolution_multiply_fusion.1
  503.9 2.9 reduce_sum.68
  508.8 3.0 gather_fusion.11
  518.3 137.8 %all-reduce.6.cloned.1.call-done = f32[128,128]{0,1:T(8,128)} async-done(((f32[128,128]{0,1:T(8,128)}), f32[128,128]{0,1:T(8,128)}) %all-reduce.6.cloned.1.call-update) | async-done | bytes 65552 | tf_op jit(solution)/shard_map/psum | solution.py:95
  657.9 11.7 %cholesky.55 = f32[128,128]{1,0:T(8,128)S(1)} custom-call(f32[128,128]{1,0:T(8,128)S(1)} %fusion.39), custom_call_target="Cholesky" | custom-call | tf_op jit(solution)/shard_map/jit(cholesky)/cholesky | solution.py:71
  670.9 9.8 %custom-call.7 = f32[1,128,128]{1,2,0:T(8,128)S(1)} custom-call(f32[1,128,128]{2,1,0:T(8,128)S(1)} %fusion.37), custom_call_target="InvertDiagBlocksLowerTriangular" | custom-call | tf_op jit(solution)/shard_map/jit(_solve_triangular)/triangular_solve | solution.py:72
  685.4 29.7 %all_to_all.40 = f32[4,1024,128]{2,1,0:T(8,128)} all-to-all(f32[4,1024,128]{2,1,0:T(8,128)S(1)} %stack.20), channel_id=1, replica_groups=mesh['dom'=32,'near'=4] {'near'}, dimensions={0} | all-to-all | bytes 4194304 | tf_op jit(solution)/shard_map/all_to_all | solution.py:28
  715.1 4.1 gather_fusion.12
  719.2 8.2 convolution_multiply_fusion
  727.4 2.9 reduce_sum.69
  732.3 3.0 gather_fusion.13
  737.2 2.8 fusion.14
  740.1 136.8 %all-reduce.8.cloned.1.call-done = f32[128,128]{0,1:T(8,128)} async-done(((f32[128,128]{0,1:T(8,128)}), f32[128,128]{0,1:T(8,128)}) %all-reduce.8.cloned.1.call-update) | async-done | bytes 65552 | tf_op jit(solution)/shard_map/psum | solution.py:99
  (118 shorter events, 69.2 us)
Async XLA Ops:
  7.2 40.6 %copy-start = (f32[48,128,128]{2,1,0:T(8,128)S(1)}, f32[48,128,128]{2,1,0:T(8,128)}, u32[]{:S(2)}) copy-start(f32[48,128,128]{2,1,0:T(8,128)} %param.12) | copy-start | bytes 9437188
  7.2 53.7 %all-gather.8.cloned.1.call-start = ((), (), s32[]{:S(2)}) async-start(), calls=%async_computation.7 | async-start | bytes 2162688 | tf_op jit(solution)/shard_map/all_gather | solution.py:38
  9.7 8.4 copy-start.13
  9.7 8.4 copy-start.14
  9.7 8.4 copy-start.15
  9.7 8.5 copy-start.16
  12.3 31.5 %all-to-all-start = ((f32[4,1024,128]{2,1,0:T(8,128)}), f32[4,1024,128]{2,1,0:T(8,128)}, u32[]{:S(2)}, u32[]{:S(2)}) async-start(f32[4,1024,128]{2,1,0:T(8,128)} %stack.14), calls=%async_computation | async-start | bytes 4194304 | tf_op jit(solution)/shard_map/all_to_all | solution.py:28
  18.1 97.2 %all-gather.10.cloned.1.call-start = ((), (), s32[]{:S(2)}) async-start(), calls=%async_computation.8 | async-start | bytes 2162688 | tf_op jit(solution)/shard_map/all_gather | solution.py:38
  65.8 0.8 copy-start.4
  67.8 0.8 copy-start.9
  69.3 100.4 %all-gather.12.cloned.1.call-start = ((), (), s32[]{:S(2)}) async-start(), calls=%async_computation.9 | async-start | bytes 2162688 | tf_op jit(solution)/shard_map/all_gather | solution.py:38
  120.3 0.8 copy-start.8
  122.5 0.8 copy-start.11
  124.1 196.7 %all-reduce.4.cloned.1.call-start = ((), (), s32[]{:S(2)}) async-start(), calls=%async_computation.10 | async-start | bytes 131072 | tf_op jit(solution)/shard_map/psum | solution.py:95
  176.3 0.8 copy-start.6
  178.8 218.1 %all-gather.14.cloned.1.call-start = ((), (), s32[]{:S(2)}) async-start(), calls=%async_computation.11 | async-start | bytes 2162688 | tf_op jit(solution)/shard_map/all_gather | solution.py:38
  347.4 0.8 copy-start.1
  348.9 104.4 %all-gather.16.cloned.1.call-start = ((), (), s32[]{:S(2)}) async-start(), calls=%async_computation.12 | async-start | bytes 2162688 | tf_op jit(solution)/shard_map/all_gather | solution.py:38
  401.8 0.8 copy-start.3
  403.8 0.8 copy-start.10
  405.3 103.5 %all-gather.18.cloned.1.call-start = ((), (), s32[]{:S(2)}) async-start(), calls=%async_computation.13 | async-start | bytes 2162688 | tf_op jit(solution)/shard_map/all_gather | solution.py:38
  458.3 0.8 copy-start.7
  460.5 0.8 copy-start.12
  462.0 194.1 %all-reduce.6.cloned.1.call-start = ((), (), s32[]{:S(2)}) async-start(), calls=%async_computation.14 | async-start | bytes 131072 | tf_op jit(solution)/shard_map/psum | solution.py:95
  515.4 0.8 copy-start.5
  517.8 214.5 %all-gather.20.cloned.1.call-start = ((), (), s32[]{:S(2)}) async-start(), calls=%async_computation.15 | async-start | bytes 2162688 | tf_op jit(solution)/shard_map/all_gather | solution.py:38
  682.7 0.8 copy-start.2
  684.2 192.7 %all-reduce.8.cloned.1.call-start = ((), (), s32[]{:S(2)}) async-start(), calls=%async_computation.16 | async-start | bytes 131072 | tf_op jit(solution)/shard_map/psum | solution.py:99
Sparse Core Ops, SparseCore 0:
  10.8 47.0 all-gather.7
  69.4 44.3 all-gather.9
  124.2 45.5 all-gather.11
  178.9 141.8 all-reduce.3
  349.0 40.6 all-gather.13
  405.4 40.6 all-gather.15
  462.1 41.1 all-gather.17
  517.9 138.0 all-reduce.5
  684.3 40.6 all-gather.19
  740.2 136.6 all-reduce.7
